TPU v7x, 32 devices: a whole 2x2x4 slice. The times are simulated.
32 devices in a mesh: ctx: 8 (over y, x, core), chan: 4 (over z).
Axes of the slice: x: 2, y: 2, z: 4, core: 2. Of those that a mesh axis runs over, the one named last changes fastest.
Arguments:
- queries: bfloat16 [1024, 4096], P('ctx', 'chan'), may hold values from -8 to 8
- key_rows: bfloat16 [1024, 4096], P('ctx', 'chan'), may hold values from -8 to 8
- value_rows: bfloat16 [1024, 4096], P('ctx', 'chan'), may hold values from -16 to 16
- gate_in: bfloat16 [1024, 4096], P('ctx', 'chan'), may hold values from -6 to 6
- gate_out: bfloat16 [1024, 4096], P('ctx', 'chan'), may hold values from -6 to 6
- kernel_taps: float32 [512, 7], P('chan'), may hold values from -2 to 2
- norm_gain: float32 [4096], P('chan'), may hold values from 0.1 to 1.9
- cotangent: bfloat16 [1024, 4096], P('ctx', 'chan'), may hold values from -6 to 6
Outputs:
- mixed: bfloat16 [1024, 4096], P('ctx', 'chan')
- grad_queries: bfloat16 [1024, 4096], P('ctx', 'chan')
- grad_keys: bfloat16 [1024, 4096], P('ctx', 'chan')
- grad_values: bfloat16 [1024, 4096], P('ctx', 'chan')
- grad_gate_in: bfloat16 [1024, 4096], P('ctx', 'chan')
- grad_gate_out: bfloat16 [1024, 4096], P('ctx', 'chan')
- grad_filter: float32 [512, 7], P('chan')
- grad_gain: float32 [4096], P('chan')
All inputs are finite; a program needn't handle non-finite values.
Results may differ from a plain program's by a relative error of at most 0.015.
Values may be sent and summed in bfloat16 or wider, within the bound.
No kernel may reach another device: no remote copies, remote signals or barrier semaphores. Data moves between devices by JAX's collectives and lax.ppermute only.
A program may use at most 128 MiB of HBM per device.

v0:
```python
import jax
import jax.numpy as jnp
from jax import lax
from jax.sharding import PartitionSpec as P

HEAD = 128
FILT = 7
WIDTH = 4096


EPS = 1e-06
NEG = -1e30


def from_behind(shard, axis, by):
    length = lax.axis_size(axis)
    pairs = [(i, i + by) for i in range(length) if 0 <= i + by < length]
    return lax.ppermute(shard, axis, pairs)


def score_block(query_heads, key_block, query_pos, key_pos):
    scores = jnp.einsum(
        "rhe,khe->hrk", query_heads, key_block, preferred_element_type=jnp.float32
    ) * HEAD ** (-0.5)
    allowed = query_pos[:, None] >= key_pos[None, :]
    return jnp.where(allowed[None], scores, NEG)


def row_totals(query_heads, query_pos, block_count, keys_heads, block_rows):
    row_count = query_heads.shape[0]
    head_count = query_heads.shape[1]

    def advance(block_index, running):
        row_max, row_sum = running
        first_key = block_index * block_rows
        key_block = lax.dynamic_slice_in_dim(keys_heads, first_key, block_rows, 0)
        key_pos = first_key + jnp.arange(block_rows, dtype=jnp.int32)
        scores = score_block(query_heads, key_block, query_pos, key_pos)
        new_max = jnp.maximum(row_max, jnp.max(scores, axis=2))
        row_sum = row_sum * jnp.exp(row_max - new_max) + jnp.sum(
            jnp.exp(scores - new_max[:, :, None]), axis=2
        )
        return (new_max, row_sum)

    initial = (
        jnp.full((head_count, row_count), NEG, jnp.float32),
        jnp.zeros((head_count, row_count), jnp.float32),
    )
    row_max, row_sum = lax.fori_loop(0, block_count, advance, initial)
    return row_max + jnp.log(row_sum)


def row_outputs(query_heads, query_pos, block_count, keys_heads, values_heads, lse, block_rows):
    row_count = query_heads.shape[0]
    head_count = query_heads.shape[1]

    def advance(block_index, summed):
        first_key = block_index * block_rows
        key_block = lax.dynamic_slice_in_dim(keys_heads, first_key, block_rows, 0)
        value_block = lax.dynamic_slice_in_dim(values_heads, first_key, block_rows, 0)
        key_pos = first_key + jnp.arange(block_rows, dtype=jnp.int32)
        scores = score_block(query_heads, key_block, query_pos, key_pos)
        weights_low = jnp.exp(scores - lse[:, :, None]).astype(jnp.bfloat16)
        return summed + jnp.einsum(
            "hrk,khe->rhe", weights_low, value_block, preferred_element_type=jnp.float32
        )

    summed = lax.fori_loop(
        0, block_count, advance, jnp.zeros((row_count, head_count, HEAD), jnp.float32)
    )
    return summed.reshape(row_count, head_count * HEAD).astype(jnp.bfloat16)


def query_grads(
    query_heads, d_heads, query_pos, block_count, keys_heads, values_heads, lse, delta, block_rows
):
    row_count = query_heads.shape[0]
    head_count = query_heads.shape[1]

    def advance(block_index, summed):
        first_key = block_index * block_rows
        key_block = lax.dynamic_slice_in_dim(keys_heads, first_key, block_rows, 0)
        value_block = lax.dynamic_slice_in_dim(values_heads, first_key, block_rows, 0)
        key_pos = first_key + jnp.arange(block_rows, dtype=jnp.int32)
        scores = score_block(query_heads, key_block, query_pos, key_pos)
        weights = jnp.exp(scores - lse[:, :, None])
        d_probs = jnp.einsum(
            "rhe,khe->hrk", d_heads, value_block, preferred_element_type=jnp.float32
        )
        d_scores = (weights * (d_probs - delta[:, :, None])).astype(jnp.bfloat16)
        return summed + jnp.einsum(
            "hrk,khe->rhe", d_scores, key_block, preferred_element_type=jnp.float32
        )

    summed = lax.fori_loop(
        0, block_count, advance, jnp.zeros((row_count, head_count, HEAD), jnp.float32)
    )
    return (summed * HEAD ** (-0.5)).reshape(row_count, head_count * HEAD).astype(jnp.bfloat16)


def shards(queries, key_rows, value_rows, gate_in, gate_out, kernel_taps, norm_gain, cotangent):
    row_count = queries.shape[0]
    channels = queries.shape[1]
    head_count = channels // HEAD
    group_count = kernel_taps.shape[0]
    devices = lax.axis_size("ctx")
    position = lax.axis_index("ctx")
    own_first = position * row_count
    total_rows = row_count * devices
    block_rows = min(512, total_rows)
    local_pos = jnp.arange(row_count, dtype=jnp.int32)
    keys_all, values_all = (
        lax.all_gather(key_rows, "ctx", axis=0, tiled=True),
        lax.all_gather(value_rows, "ctx", axis=0, tiled=True),
    )
    keys_heads = keys_all.reshape(total_rows, head_count, HEAD)
    query_sets = (queries, own_first + local_pos)
    query_block, query_pos = query_sets
    block_count = query_pos[-1] // block_rows + 1
    lse_sets = row_totals(
        query_block.reshape(-1, head_count, HEAD), query_pos, block_count, keys_heads, block_rows
    )
    values_heads = values_all.reshape(total_rows, head_count, HEAD)
    query_block, query_pos = query_sets
    outputs = row_outputs(
        query_block.reshape(-1, head_count, HEAD),
        query_pos,
        block_count,
        keys_heads,
        values_heads,
        lse_sets,
        block_rows,
    )
    lse_rows = lse_sets.T
    attn_wide = outputs.astype(jnp.float32)
    square_sum = lax.psum(jnp.sum(attn_wide * attn_wide, axis=1), "chan")
    inverse_rms = 1.0 / jnp.sqrt(square_sum / WIDTH + EPS)
    normed = attn_wide * inverse_rms[:, None] * norm_gain[None, :]
    gate_wide = gate_in.astype(jnp.float32)
    mixed_in = gate_wide * normed
    taps = jnp.broadcast_to(
        kernel_taps[:, None, :], (group_count, channels // group_count, FILT)
    ).reshape(channels, FILT)
    rim_before = from_behind(mixed_in[row_count - (FILT - 1) :], "ctx", 1)
    extended = jnp.concatenate([rim_before, mixed_in], axis=0)
    conv_out = jnp.zeros((row_count, channels), jnp.float32)
    for lag in range(FILT):
        conv_out = (
            conv_out + taps[:, lag][None, :] * extended[FILT - 1 - lag : FILT - 1 - lag + row_count]
        )
    out_gate = gate_out.astype(jnp.float32)
    mixed = (out_gate * conv_out).astype(jnp.bfloat16)
    upstream = cotangent.astype(jnp.float32)
    grad_gate_out = (upstream * conv_out).astype(jnp.bfloat16)
    d_conv = upstream * out_gate
    tap_columns = []
    for lag in range(FILT):
        per_channel = jnp.sum(
            d_conv * extended[FILT - 1 - lag : FILT - 1 - lag + row_count], axis=0
        )
        tap_columns.append(per_channel.reshape(group_count, -1).sum(axis=1))
    tap_terms = jnp.stack(tap_columns, axis=1)
    rim_after = from_behind(d_conv[: FILT - 1], "ctx", -1)
    extended_grad = jnp.concatenate([d_conv, rim_after], axis=0)
    d_mixed = jnp.zeros((row_count, channels), jnp.float32)
    for lag in range(FILT):
        d_mixed = d_mixed + taps[:, lag][None, :] * extended_grad[lag : lag + row_count]
    grad_gate_in = (d_mixed * normed).astype(jnp.bfloat16)
    d_normed = d_mixed * gate_wide
    gain_terms = jnp.sum(d_normed * attn_wide * inverse_rms[:, None], axis=0)
    grad_filter, grad_gain = lax.psum((tap_terms, gain_terms), "ctx")
    scaled = d_normed * norm_gain[None, :]
    row_dot = lax.psum(jnp.sum(scaled * attn_wide, axis=1), "chan")
    d_attn = (
        inverse_rms[:, None] * scaled - attn_wide * (inverse_rms**3 * row_dot / WIDTH)[:, None]
    ).astype(jnp.bfloat16)
    d_heads = d_attn.reshape(row_count, head_count, HEAD)
    delta_rows = jnp.sum(
        d_heads.astype(jnp.float32) * attn_wide.reshape(row_count, head_count, HEAD), axis=2
    )
    own_count = (own_first + row_count - 1) // block_rows + 1
    grad_queries = query_grads(
        queries.reshape(row_count, head_count, HEAD),
        d_heads,
        own_first + local_pos,
        own_count,
        keys_heads,
        values_heads,
        lse_rows.T,
        delta_rows.T,
        block_rows,
    )
    lse_all, delta_all = (
        lax.all_gather(lse_rows, "ctx", axis=0, tiled=True),
        lax.all_gather(delta_rows, "ctx", axis=0, tiled=True),
    )
    own_keys = key_rows.reshape(row_count, head_count, HEAD)
    own_values = value_rows.reshape(row_count, head_count, HEAD)
    key_pos = own_first + local_pos
    empty_grad = jnp.zeros((row_count, head_count, HEAD), jnp.float32)
    query_piece = lax.all_gather(queries, "ctx", axis=0, tiled=True)
    d_piece = lax.all_gather(d_attn, "ctx", axis=0, tiled=True)
    piece_rows = query_piece.shape[0]

    def contribute(totals):
        query_heads = query_piece.reshape(piece_rows, head_count, HEAD)
        piece_heads = d_piece.reshape(piece_rows, head_count, HEAD)
        query_pos = jnp.arange(piece_rows, dtype=jnp.int32)
        lse_piece = lse_all.T
        delta_piece = delta_all.T
        scores = score_block(query_heads, own_keys, query_pos, key_pos)
        weights = jnp.exp(scores - lse_piece[:, :, None])
        d_probs = jnp.einsum(
            "rhe,khe->hrk", piece_heads, own_values, preferred_element_type=jnp.float32
        )
        d_scores = (weights * (d_probs - delta_piece[:, :, None])).astype(jnp.bfloat16)
        key_grad = jnp.einsum(
            "hrk,rhe->khe", d_scores, query_heads, preferred_element_type=jnp.float32
        )
        value_grad = jnp.einsum(
            "hrk,rhe->khe",
            weights.astype(jnp.bfloat16),
            piece_heads,
            preferred_element_type=jnp.float32,
        )
        return (key_grad, value_grad)

    def unchanged(totals):
        return totals

    key_grad, value_grad = lax.cond(
        jnp.int32(0) + piece_rows > own_first, contribute, unchanged, (empty_grad, empty_grad)
    )
    grad_keys = (key_grad * HEAD ** (-0.5)).reshape(row_count, channels).astype(jnp.bfloat16)
    grad_values = value_grad.reshape(row_count, channels).astype(jnp.bfloat16)
    return (
        mixed,
        grad_queries,
        grad_keys,
        grad_values,
        grad_gate_in,
        grad_gate_out,
        grad_filter,
        grad_gain,
    )


def solution(mesh):
    placed = (
        P("ctx", "chan"),
        P("ctx", "chan"),
        P("ctx", "chan"),
        P("ctx", "chan"),
        P("ctx", "chan"),
        P("chan", None),
        P("chan"),
        P("ctx", "chan"),
    )
    return jax.shard_map(
        shards,
        mesh=mesh,
        in_specs=placed,
        out_specs=(
            P("ctx", "chan"),
            P("ctx", "chan"),
            P("ctx", "chan"),
            P("ctx", "chan"),
            P("ctx", "chan"),
            P("ctx", "chan"),
            P("chan", None),
            P("chan"),
        ),
        check_vma=False,
    )
```

profile of v0, /device:TPU:0, one launch (start us, length us, event | category | flops | bytes accessed | tf_op | source)
XLA Modules:
  0.0 189.7 jit_solution(9424736942254590684)
XLA Ops:
  7.2 1.8 copy.75
  9.1 1.8 copy.74
  11.0 1.1 convert_multiply_fusion.1
  12.1 0.8 copy-done.3
  12.9 1.3 collective-permute-start.1
  14.3 0.6 slice.80
  16.8 0.2 copy.76
  17.7 0.2 copy.80
  17.9 0.2 broadcast_in_dim.76
  18.1 0.2 reshape.211
  18.3 23.0 %all-gather.7.cloned.1.call-done = bf16[1024,1024]{0,1:T(8,128)(2,1)} async-done(((bf16[128,1024]{0,1:T(8,128)(2,1)}), bf16[1024,1024]{0,1:T(8,128)(2,1)}) %all-gather.7.cloned.1.call-update) | async-done | bytes 2097168 | tf_op jit(solution)/shard_map/all_gather | solution.py:113
  41.3 3.0 %copy.79 = bf16[1024,8,128]{2,0,1:T(8,128)(2,1)S(1)} copy(bf16[1024,8,128]{0,2,1:T(8,128)(2,1)} %bitcast.151) | data formatting | bytes 4194304
  44.4 1.2 while.35
  44.4 0.1 broadcast_compare_fusion.6
  44.6 0.5 fusion.130
  45.1 0.4 exponential_reduce_fusion.2
  45.6 26.3 %all-gather.5.cloned.1.call-done = bf16[1024,1024]{0,1:T(8,128)(2,1)} async-done(((bf16[128,1024]{0,1:T(8,128)(2,1)}), bf16[1024,1024]{0,1:T(8,128)(2,1)}) %all-gather.5.cloned.1.call-update) | async-done | bytes 2097168 | tf_op jit(solution)/shard_map/all_gather | solution.py:114
  71.9 2.4 %while.36 = (s32[]{:T(128)}, f32[128,8,128]{0,2,1:T(8,128)S(1)}, s32[]{:T(128)}, bf16[1024,8,128]{0,2,1:T(8,128)(2,1)}, bf16[1024,8,128]{2,0,1:T(8,128)(2,1)S(1)...) while((s32[]{:T(128)}, f32[128,8,128]{0,2,1:T(8,128)S(1)}, ...), condition=%wide.region_5.6_spmd.clone, body=%wide.region_4.5_spmd.clone.sunk | while | flops 270729856 | bytes 3549363 | solution.py:68
  72.0 0.1 broadcast_compare_fusion.7
  72.1 2.2 %fusion.134 = f32[128,8,128]{0,2,1:T(8,128)S(1)} fusion(f32[128,8,128]{0,2,1:T(8,128)S(1)} %get-tuple-element.657, bf16[128,8,128]{2,0,1:T(8,128)(2,1)S(1)} %get-tuple-element.673, f32[8,128]{1,0:T(8,128)S(1)} %get-tuple-element.674, bf16[1024,8,128]{2,0,1:T(8,128)(2,1)S(1)} %get-tuple-element.672, s32[]{:T(128)S(6)} %select_n.93, ...), kind=kOutput, calls=%fused_computation.44.clone.1 | convolution fusion | flops 270663680 | bytes 3478528 | tf_op jit(solution)/shard_map/while/body/hrk,khe->rhe/dot_general | solution.py:64
  74.4 1.0 multiply_reduce_fusion.10
  75.3 11.7 %psum.28 = f32[128]{0:T(128)S(1)} all-reduce(f32[128]{0:T(128)S(1)} %get-tuple-element.441), channel_id=1, replica_groups=mesh['ctx'=8,'chan'=4] {'chan'}, use_global_device_ids=true, to_apply=%region_7.8 | all-reduce | flops 128 | bytes 1024 | tf_op jit(solution)/shard_map/psum | solution.py:136
  87.0 1.2 copy.97
  88.3 4.0 %multiply_convert_fusion.1 = (bf16[128,1024]{1,0:T(8,128)(2,1)}, f32[128,1024]{1,0:T(8,128)S(1)}) fusion(f32[128,1024]{1,0:T(8,128)S(1)} %copy.97, f32[1024]{0:T(1024)S(1)} %copy-done.10, f32[128]{0:T(128)S(1)} %add_rsqrt_fusion, f32[6,1024]{1,0:T(8,128)S(1)} %collective-permute-done.1, f32[128,1024]{1,0:T(8,128)} %copy-done.3, f32[1024]{0:T(1024)S(1)} %bitcast.162, ...), kind=kLoop, calls=%fused_computation.133 | loop fusion | flops 3014656 | bytes 1892864 | tf_op jit(solution)/shard_map/convert_element_type | solution.py:168
  92.3 0.8 copy-done.1
  93.1 0.2 multiply_reduce_fusion
  93.3 8.4 %psum.29 = f32[128]{0:T(128)S(1)} all-reduce(f32[128]{0:T(128)S(1)} %get-tuple-element.373), channel_id=1, replica_groups=mesh['ctx'=8,'chan'=4] {'chan'}, use_global_device_ids=true, to_apply=%region_9.10 | all-reduce | flops 128 | bytes 1024 | tf_op jit(solution)/shard_map/psum | solution.py:173
  101.7 2.0 %subtract_convert_fusion = (bf16[128,1024]{1,0:T(8,128)(2,1)}, f32[128,1024]{1,0:T(8,128)S(1)}) fusion(f32[128,1024]{1,0:T(8,128)S(1)} %copy.97, f32[128]{0:T(128)S(1)} %fusion.102, f32[1024]{0:T(1024)S(1)} %copy-done.10, f32[128]{0:T(128)S(1)} %add_rsqrt_fusion, f32[128,1024]{1,0:T(8,128)} %copy-done.1, bf16[128,1024]{1,0:T(8,128)(2,1)} %param.19), kind=kLoop, calls=%fused_computation.137 | loop fusion | flops 1310720 | bytes 2102272 | tf_op jit(solution)/shard_map/convert_element_type | solution.py:176
  103.8 0.6 slice.103
  104.4 1.3 collective-permute-start
  105.7 1.0 copy.109
  106.7 0.2 copy.82
  106.9 1.1 multiply_reduce_fusion.8
  108.0 1.0 copy_bitcast_fusion
  109.0 0.9 broadcast.128
  109.9 5.9 %while.37 = (s32[]{:T(128)}, f32[128,8,128]{0,2,1:T(8,128)}, s32[]{:T(128)}, bf16[1024,8,128]{2,0,1:T(8,128)(2,1)S(1)}, bf16[128,8,128]{2,0,1:T(8,128)(2,1)S(1)}...) while((s32[]{:T(128)}, f32[128,8,128]{0,2,1:T(8,128)}, ...), condition=%wide.region_12.13_spmd.clone, body=%wide.region_11.12_spmd.clone.sunk | while | flops 405996160 | bytes 9058503 | solution.py:95
  109.9 1.7 fusion.140
  111.7 0.1 broadcast_compare_fusion.8
  111.8 4.1 %fusion.141 = f32[128,8,128]{0,2,1:T(8,128)} fusion(f32[128,8,128]{0,2,1:T(8,128)} %get-tuple-element.695, f32[8,512,128]{2,1,0:T(8,128)} %fusion.140, bf16[128,8,128]{2,0,1:T(8,128)(2,1)S(1)} %get-tuple-element.715, f32[8,128]{1,0:T(8,128)S(1)} %get-tuple-element.716, bf16[1024,8,128]{0,2,1:T(8,128)(2,1)} %get-tuple-element.714, s32[]{:T(128)S(6)} %select_n.95, ...), kind=kOutput, calls=%fused_computation.64.clone.1 | convolution fusion | flops 271712256 | bytes 5579776 | tf_op jit(solution)/shard_map/while/body/hrk,khe->rhe/dot_general | solution.py:91
  115.9 1.1 multiply_convert_fusion.3
  117.0 0.9 copy.98
  117.9 17.9 %all_gather.23 = f32[1024,8]{0,1:T(8,128)S(1)} all-gather(f32[128,8]{0,1:T(8,128)S(1)} %bitcast.178), channel_id=1, replica_groups=mesh['ctx'=8,'chan'=4] {'ctx'}, dimensions={0}, use_global_device_ids=true | all-gather | bytes 36864 | tf_op jit(solution)/shard_map/all_gather | solution.py:195
  135.8 8.5 %all_gather.21 = f32[1024,8]{0,1:T(8,128)S(1)} all-gather(f32[128,8]{0,1:T(8,128)S(1)} %bitcast.179), channel_id=1, replica_groups=mesh['ctx'=8,'chan'=4] {'ctx'}, dimensions={0}, use_global_device_ids=true | all-gather | bytes 36864 | tf_op jit(solution)/shard_map/all_gather | solution.py:194
  144.3 1.2 fusion.78
  145.5 1.2 multiply_reduce_fusion.1
  146.9 0.1 reshape.218
  147.0 0.1 reshape.219
  147.4 0.1 reduce_sum.175
  147.5 0.1 reduce_sum.177
  147.6 0.1 reduce_sum.179
  147.7 0.1 reduce_sum.181
  147.8 0.1 reduce_sum.183
  148.0 0.1 reduce_sum.185
  148.1 0.1 reduce_sum.187
  148.2 14.2 %all-reduce = (f32[128,7]{0,1:T(8,128)}, f32[1024]{0:T(1024)}) all-reduce(f32[128,7]{0,1:T(8,128)S(1)} %stack.31, f32[1024]{0:T(1024)S(1)} %get-tuple-element.372), channel_id=1, replica_groups=mesh['ctx'=8,'chan'=4] {'ctx'}, use_global_device_ids=true, to_apply=%region_29.30 | all-reduce | flops 1920 | bytes 15360 | tf_op jit(solution)/shard_map/psum | solution.py:171
  162.5 19.8 %conditional.1 = (f32[128,8,128]{0,2,1:T(8,128)S(1)}, bf16[128,1024]{1,0:T(8,128)(2,1)}) conditional(s32[]{:T(128)} %convert_element_type.91, () %tuple.33, (s32[128]{0:T(128)S(1)}, bf16[1024,1024]{1,0:T(8,128)(2,1)}, bf16[128,1024]{1,0:T(8,128)(2,1)S(1)}, f32[1024,8]{0,1:T(8,128)S(1)}, bf16[1024,1024]{1,0:T(8,128)(2,1)}, ...), branch_computations={%region_13.14_spmd, %region_14.15_spmd} | conditional | flops 1084489728 | bytes 38503096 | solution.py:231
  162.5 4.3 %fusion.11 = f32[8,1024,128]{2,1,0:T(8,128)} fusion(bf16[1024,1024]{1,0:T(8,128)(2,1)} %get-tuple-element.149, bf16[128,1024]{1,0:T(8,128)(2,1)S(1)} %get-tuple-element.150), kind=kOutput, calls=%fused_computation.9 | convolution fusion | flops 268435456 | bytes 6553600 | tf_op jit(solution)/shard_map/cond/branch_1_fun/rhe,khe->hrk/dot_general | solution.py:22
  166.8 4.1 %copy.88 = bf16[1024,1024]{0,1:T(8,128)(2,1)} copy(bf16[1024,1024]{1,0:T(8,128)(2,1)} %get-tuple-element.359) | data formatting | bytes 4194304 | tf_op jit(solution)/shard_map
  170.9 0.1 iota_compare_fusion
  171.0 6.4 %fusion.19 = f32[128,8,128]{2,0,1:T(8,128)S(1)} fusion(f32[8,1024,128]{2,1,0:T(8,128)} %fusion.11, bf16[1024,8,128]{0,2,1:T(8,128)(2,1)} %bitcast.152, f32[8,1024]{1,0:T(8,128)S(1)} %bitcast.174, f32[8,1024]{1,0:T(8,128)S(1)} %bitcast.176, pred[1024,128]{1,0:T(8,128)(4,1)S(1)} %iota_compare_fusion, bf16[1024,1024]{1,0:T(8,128)(2,1)S(1)} %copy-done.4, ...), kind=kOutput, calls=%fused_computation.17 | convolution fusion | flops 543162368 | bytes 9371648 | tf_op jit(solution)/shard_map/cond/branch_1_fun/hrk,rhe->khe/dot_general | solution.py:217
  177.4 0.2 copy.101
  177.6 3.8 %fusion.22 = bf16[8,128,128]{1,2,0:T(8,128)(2,1)S(1)} fusion(bf16[1024,8,128]{0,2,1:T(8,128)(2,1)} %bitcast.153, f32[8,1024,128]{2,1,0:T(8,128)} %fusion.11, f32[8,1024]{1,0:T(8,128)} %bitcast.175, pred[1024,128]{1,0:T(8,128)(4,1)S(1)} %iota_compare_fusion), kind=kOutput, calls=%fused_computation.18 | convolution fusion | flops 272760832 | bytes 6717440 | tf_op jit(solution)/shard_map/cond/branch_1_fun/hrk,rhe->khe/dot_general | solution.py:220
  181.4 0.9 copy.103
  182.3 0.9 copy.99
  (67 shorter events, 0.9 us)
Async XLA Ops:
  7.2 9.7 %copy-start.6 = (bf16[128,1024]{1,0:T(8,128)(2,1)S(1)}, bf16[128,1024]{1,0:T(8,128)(2,1)}, u32[]{:S(2)}) copy-start(bf16[128,1024]{1,0:T(8,128)(2,1)} %param.16) | copy-start | bytes 786436
  7.2 10.7 %copy-start.15 = (f32[128,7]{0,1:T(8,128)S(1)}, f32[128,7]{0,1:T(8,128)}, u32[]{:S(2)}) copy-start(f32[128,7]{0,1:T(8,128)} %param.21) | copy-start | bytes 10756
  7.2 34.1 %all-gather.7.cloned.1.call-start = ((), (), s32[]{:S(2)}) async-start(), calls=%async_computation.1 | async-start | bytes 2359296 | tf_op jit(solution)/shard_map/all_gather | solution.py:113
  9.1 62.8 %all-gather.5.cloned.1.call-start = ((), (), s32[]{:S(2)}) async-start(), calls=%async_computation | async-start | bytes 2359296 | tf_op jit(solution)/shard_map/all_gather | solution.py:114
  10.9 151.5 %all-gather.9.cloned.1.call-start = ((), (), s32[]{:S(2)}) async-start(), calls=%async_computation.2 | async-start | bytes 2359296 | tf_op jit(solution)/shard_map/all_gather | solution.py:201
  12.1 0.8 copy-start.3
  12.9 75.4 %collective-permute-start.1 = (f32[6,1024]{1,0:T(8,128)S(1)}, f32[6,1024]{1,0:T(8,128)S(1)}, u32[]{:S(2)}, u32[]{:S(2)}) collective-permute-start(f32[6,1024]{1,0:T(8,128)S(1)} %slice.119), channel_id=1, source_target_pairs={{4,0},{8,4},{12,8},{16,12},{20,16},{24,20},{28,24},{5,1},{9,5},{13... | collective-permute-start | bytes 73736 | tf_op jit(solution)/shard_map/ppermute | solution.py:18
  14.2 148.2 %all-gather.11.cloned.1.call-start = ((), (), s32[]{:S(2)}) async-start(), calls=%async_computation.3 | async-start | bytes 2359296 | tf_op jit(solution)/shard_map/all_gather | solution.py:202
  74.3 19.0 %copy-start = (f32[128,8,128]{0,2,1:T(8,128)}, f32[128,8,128]{0,2,1:T(8,128)S(1)}, u32[]{:S(2)}) copy-start(f32[128,8,128]{0,2,1:T(8,128)S(1)} %get-tuple-element.171) | copy-start | bytes 1572868
  74.4 13.9 %copy-start.10 = (f32[1024]{0:T(1024)S(1)}, f32[1024]{0:T(1024)}, u32[]{:S(2)}) copy-start(f32[1024]{0:T(1024)} %param.22) | copy-start | bytes 12292
  88.3 4.9 %copy-start.7 = (bf16[128,1024]{1,0:T(8,128)(2,1)S(1)}, bf16[128,1024]{1,0:T(8,128)(2,1)}, u32[]{:S(2)}) copy-start(bf16[128,1024]{1,0:T(8,128)(2,1)} %param.19) | copy-start | bytes 786436
  92.3 0.8 copy-start.1
  104.4 39.9 %collective-permute-start = (f32[6,1024]{1,0:T(8,128)}, f32[6,1024]{1,0:T(8,128)S(1)}, u32[]{:S(2)}, u32[]{:S(2)}) collective-permute-start(f32[6,1024]{1,0:T(8,128)} %slice.103), channel_id=1, source_target_pairs={{0,4},{4,8},{8,12},{12,16},{16,20},{20,24},{24,28},{1,5},{5,9},{9,... | collective-permute-start | bytes 73736 | tf_op jit(solution)/shard_map/ppermute | solution.py:18
  109.9 34.4 %copy-start.2 = (bf16[128,1024]{1,0:T(8,128)(2,1)S(1)}, bf16[128,1024]{1,0:T(8,128)(2,1)}, u32[]{:S(2)}) copy-start(bf16[128,1024]{1,0:T(8,128)(2,1)} %param.23) | copy-start | bytes 786436
  115.9 29.6 %copy-start.8 = (bf16[128,1024]{1,0:T(8,128)(2,1)S(1)}, bf16[128,1024]{1,0:T(8,128)(2,1)}, u32[]{:S(2)}) copy-start(bf16[128,1024]{1,0:T(8,128)(2,1)} %param.20) | copy-start | bytes 786436
  144.3 18.1 %copy-start.5 = (bf16[128,1024]{1,0:T(8,128)(2,1)S(1)}, bf16[128,1024]{1,0:T(8,128)(2,1)}, u32[]{:S(2)}) copy-start(bf16[128,1024]{1,0:T(8,128)(2,1)} %param.17) | copy-start | bytes 786436
  162.5 4.3 %copy-start.11 = (f32[1024,8]{0,1:T(8,128)}, f32[1024,8]{0,1:T(8,128)S(1)}, u32[]{:S(2)}) copy-start(f32[1024,8]{0,1:T(8,128)S(1)} %get-tuple-element.154) | copy-start | bytes 98308 | tf_op jit(solution)/shard_map/cond
  162.5 4.3 %copy-start.13 = (f32[1024,8]{0,1:T(8,128)}, f32[1024,8]{0,1:T(8,128)S(1)}, u32[]{:S(2)}) copy-start(f32[1024,8]{0,1:T(8,128)S(1)} %get-tuple-element.151) | copy-start | bytes 98308 | tf_op jit(solution)/shard_map/cond
  166.7 4.2 %copy-start.4 = (bf16[1024,1024]{1,0:T(8,128)(2,1)S(1)}, bf16[1024,1024]{1,0:T(8,128)(2,1)}, u32[]{:S(2)}) copy-start(bf16[1024,1024]{1,0:T(8,128)(2,1)} %get-tuple-element.149) | copy-start | bytes 6291460 | tf_op jit(solution)/shard_map/cond
  166.7 4.2 %copy-start.9 = (bf16[128,1024]{1,0:T(8,128)(2,1)S(1)}, bf16[128,1024]{1,0:T(8,128)(2,1)}, u32[]{:S(2)}) copy-start(bf16[128,1024]{1,0:T(8,128)(2,1)} %get-tuple-element.153) | copy-start | bytes 786436 | tf_op jit(solution)/shard_map/cond
  166.7 4.2 %copy-start.12 = (f32[1024,8]{0,1:T(8,128)S(1)}, f32[1024,8]{0,1:T(8,128)}, u32[]{:S(2)}) copy-start(f32[1024,8]{0,1:T(8,128)} %copy-done.11) | copy-start | bytes 98308 | tf_op jit(solution)/shard_map/cond
  166.8 4.2 %copy-start.14 = (f32[1024,8]{0,1:T(8,128)S(1)}, f32[1024,8]{0,1:T(8,128)}, u32[]{:S(2)}) copy-start(f32[1024,8]{0,1:T(8,128)} %copy-done.13) | copy-start | bytes 98308 | tf_op jit(solution)/shard_map/cond
Sparse Core Ops, SparseCore 0:
  10.4 30.8 all-gather.6
  43.8 28.0 all-gather.4
  73.8 27.7 all-gather.8
  109.2 30.4 all-gather.10
where the time goes:
time: 190 us
  blocking collectives  60.7 us (32%)
  waiting for transfers between devices  49.4 us (26%)
  matrix products  22.9 us (12%)
  local copies, waits for them, and re-layouts  22.2 us (12%)
  between operations  16.7 us (9%)
  other arithmetic  14.8 us (8%)
  starting transfers between devices  2.72 us (1%)
    all_gather x1, waiting for transfers between devices, shards(): lax.all_gather(value_rows, 'ctx', axis=0, tiled=True)  26.3 us
    all_gather x1, waiting for transfers between devices, shards(): lax.all_gather(key_rows, 'ctx', axis=0, tiled=True)  23 us
    all_gather x1, blocking collectives, shards(): lax.all_gather(delta_rows, 'ctx', axis=0, tiled=True)  17.9 us
    psum x1, blocking collectives, shards(): grad_filter, grad_gain = lax.psum((tap_terms, gain_terms), 'ctx')  14.2 us
    psum x1, blocking collectives, shards(): square_sum = lax.psum(jnp.sum(attn_wide * attn_wide, axis=1), 'chan')  11.7 us
    unnamed x27, local copies, waits for them, and re-layouts  10.6 us
    all_gather x1, blocking collectives, shards(): lax.all_gather(lse_rows, 'ctx', axis=0, tiled=True)  8.53 us
    psum x1, blocking collectives, shards(): row_dot = lax.psum(jnp.sum(scaled * attn_wide, axis=1), 'chan')  8.37 us
  transfers between devices with their start and end apart: 6, of which 2 were waited for; matrix products, arithmetic and copies ran while one was open for 19% of the time, Pallas kernels for 0%

commit v1 on v0

--- a/solution.py
+++ b/solution.py
@@ -1,6 +1,10 @@
+import functools
+
 import jax
 import jax.numpy as jnp
 from jax import lax
+from jax.experimental import pallas as pl
+from jax.experimental.pallas import tpu as pltpu
 from jax.sharding import PartitionSpec as P
 
 HEAD = 128
@@ -98,7 +102,7 @@
     return (summed * HEAD ** (-0.5)).reshape(row_count, head_count * HEAD).astype(jnp.bfloat16)
 
 
-def shards(queries, key_rows, value_rows, gate_in, gate_out, kernel_taps, norm_gain, cotangent):
+def shards_by_rows(queries, key_rows, value_rows, gate_in, gate_out, kernel_taps, norm_gain, cotangent):
     row_count = queries.shape[0]
     channels = queries.shape[1]
     head_count = channels // HEAD
@@ -245,6 +249,252 @@
     )
 
 
+LOG2E = 1.4426950408889634
+VMEM_LIMIT = 56 * 1024 * 1024
+
+
+def vmem_call(body, outs, scratch=(), flops=0, **extra):
+    return pl.pallas_call(
+        body,
+        out_shape=tuple(outs),
+        scratch_shapes=list(scratch),
+        compiler_params=pltpu.CompilerParams(vmem_limit_bytes=VMEM_LIMIT),
+        **extra,
+    )
+
+
+def dot_nt(a, b, precision=None):
+    return lax.dot_general(
+        a, b, (((1,), (1,)), ((), ())), precision=precision, preferred_element_type=jnp.float32
+    )
+
+
+def dot_nn(a, b):
+    return lax.dot_general(a, b, (((1,), (0,)), ((), ())), preferred_element_type=jnp.float32)
+
+
+def row_sums_as_lanes(product):
+    ones = jnp.ones((8, product.shape[1]), jnp.float32)
+    return dot_nt(ones, product, lax.Precision.HIGHEST)[0:1]
+
+
+def channel_taps(taps_ref, head, groups):
+    mine = taps_ref[pl.ds(pl.multiple_of(head * groups, 8), groups), :]
+    group_of = lax.broadcasted_iota(jnp.int32, (groups, HEAD), 1) // (HEAD // groups)
+    spread = (group_of == lax.broadcasted_iota(jnp.int32, (groups, HEAD), 0)).astype(jnp.float32)
+    return lax.dot_general(
+        mine,
+        spread,
+        (((0,), (0,)), ((), ())),
+        precision=lax.Precision.HIGHEST,
+        preferred_element_type=jnp.float32,
+    )
+
+
+def pack_body(q_ref, k_ref, v_ref, gi_ref, go_ref, ct_ref, out_ref):
+    rows = q_ref.shape[0]
+    for head in range(out_ref.shape[0]):
+        cols = slice(head * HEAD, (head + 1) * HEAD)
+        for at, ref in enumerate((q_ref, k_ref, v_ref, gi_ref)):
+            out_ref[head, at * rows : (at + 1) * rows, :] = ref[:, cols]
+        d_conv = go_ref[:, cols].astype(jnp.float32) * ct_ref[:, cols].astype(jnp.float32)
+        out_ref[head, 4 * rows : 5 * rows, :] = d_conv.astype(jnp.bfloat16)
+
+
+def forward_body(axis, rx_ref, taps_ref, gain_ref, p_ref, attn_ref, dz_ref, pay_ref, du_pad, sums):
+    blocks = rx_ref.shape[0]
+    rows = rx_ref.shape[1] // 5
+    tokens = blocks * rows
+    wide = 2 * rows if blocks % 2 == 0 else rows
+    per = wide // rows
+    head = lax.axis_index(axis)
+    groups = taps_ref.shape[0] // blocks
+    taps = channel_taps(taps_ref, head, groups)
+    gain = gain_ref[pl.ds(head, 1), :]
+
+    def part(at, first, count):
+        return rx_ref[first : first + count, at * rows : (at + 1) * rows, :].reshape(count * rows, HEAD)
+
+    v_t = part(2, 0, blocks).astype(jnp.float32).T.astype(jnp.bfloat16)
+    for b in range(blocks):
+        du_pad[b * rows : (b + 1) * rows, :] = part(4, b, 1).astype(jnp.float32)
+    du_pad[tokens : tokens + 8, :] = jnp.zeros((8, HEAD), jnp.float32)
+    scale = HEAD ** (-0.5) * LOG2E
+    for i in range(tokens // wide):
+        keys = (i + 1) * wide
+        q_i = part(0, i * per, per)
+        s = dot_nt(part(1, 0, (i + 1) * per), q_i)
+        key_pos = lax.broadcasted_iota(jnp.int32, (wide, wide), 0)
+        query_pos = lax.broadcasted_iota(jnp.int32, (wide, wide), 1)
+        edge = jnp.where(key_pos <= query_pos, s[keys - wide :], NEG)
+        s = edge if i == 0 else jnp.concatenate([s[: keys - wide], edge], axis=0)
+        top = jnp.max(s, axis=0, keepdims=True)
+        e = jnp.exp2((s - top) * scale)
+        p = (e * (1.0 / jnp.sum(e, axis=0, keepdims=True))).astype(jnp.bfloat16)
+        p_ref[:keys, i * wide : (i + 1) * wide] = p
+        attn_t = dot_nn(v_t[:, :keys], p).astype(jnp.bfloat16).astype(jnp.float32)
+        squares = jnp.sum(attn_t * attn_t, axis=0, keepdims=True)
+        attn = attn_t.T
+        first = i * wide
+        attn_ref[first : first + wide, :] = attn.astype(jnp.bfloat16)
+        dz = jnp.zeros((wide, HEAD), jnp.float32)
+        for lag in range(FILT):
+            dz = dz + taps[lag : lag + 1, :] * du_pad[first + lag : first + lag + wide, :]
+        dz_ref[first : first + wide, :] = dz
+        scaled = dz * part(3, i * per, per).astype(jnp.float32) * gain
+        dots = row_sums_as_lanes(scaled * attn)
+        for j in range(per):
+            at = i * per + j
+            sums[at : at + 1, :] = squares[:, j * rows : (j + 1) * rows]
+            sums[blocks + at : blocks + at + 1, :] = dots[:, j * rows : (j + 1) * rows]
+    low = sums[...].astype(jnp.bfloat16)
+    for d in range(pay_ref.shape[0]):
+        pay_ref[d] = low
+
+
+def backward_body(
+    axis, width, rs_ref, rx_ref, taps_ref, gain_ref, p_ref, attn_ref, dz_ref, out_ref, z_pad, ds_ref, da_ref, dl_ref
+):
+    blocks = rx_ref.shape[0]
+    rows = rx_ref.shape[1] // 5
+    tokens = blocks * rows
+    wide = 2 * rows if blocks % 2 == 0 else rows
+    per = wide // rows
+    head = lax.axis_index(axis)
+    groups = taps_ref.shape[0] // blocks
+    taps = channel_taps(taps_ref, head, groups)
+    gain = gain_ref[pl.ds(head, 1), :]
+
+    def part(at, first, count):
+        return rx_ref[first : first + count, at * rows : (at + 1) * rows, :].reshape(count * rows, HEAD)
+
+    totals = jnp.sum(rs_ref[...].astype(jnp.float32), axis=0)
+    rstd_lanes = 1.0 / jnp.sqrt(totals[:blocks] / width + EPS)
+    pull_lanes = rstd_lanes * rstd_lanes * rstd_lanes * totals[blocks:] / width
+    z_pad[0:8, :] = jnp.zeros((8, HEAD), jnp.float32)
+    grads = [jnp.zeros((1, HEAD), jnp.float32) for _ in range(FILT + 1)]
+    for b in range(blocks):
+        first = b * rows
+        rstd = jnp.broadcast_to(rstd_lanes[b : b + 1], (HEAD, rows)).T
+        pull = jnp.broadcast_to(pull_lanes[b : b + 1], (HEAD, rows)).T
+        attn = attn_ref[first : first + rows, :].astype(jnp.float32)
+        dz = dz_ref[first : first + rows, :]
+        gi = part(3, b, 1).astype(jnp.float32)
+        du = part(4, b, 1).astype(jnp.float32)
+        normed = attn * rstd * gain
+        z_pad[8 + first : 8 + first + rows, :] = gi * normed
+        conv = jnp.zeros((rows, HEAD), jnp.float32)
+        for lag in range(FILT):
+            z = z_pad[8 + first - lag : 8 + first - lag + rows, :]
+            conv = conv + taps[lag : lag + 1, :] * z
+            grads[lag] = grads[lag] + jnp.sum(du * z, axis=0, keepdims=True)
+        d_normed = dz * gi
+        grads[FILT] = grads[FILT] + jnp.sum(d_normed * attn * rstd, axis=0, keepdims=True)
+        d_attn = (rstd * (d_normed * gain) - attn * pull).astype(jnp.bfloat16)
+        da_ref[first : first + rows, :] = d_attn
+        dl_ref[0:1, first : first + rows] = row_sums_as_lanes(d_attn.astype(jnp.float32) * attn)
+        out_ref[b, 3 * rows : 4 * rows, :] = conv.astype(jnp.bfloat16)
+        out_ref[b, 4 * rows : 5 * rows, :] = (dz * normed).astype(jnp.bfloat16)
+    both = jnp.concatenate(grads, axis=0)
+    high = both.astype(jnp.bfloat16).astype(jnp.float32)
+    both = jnp.concatenate([high, both - high], axis=0).astype(jnp.bfloat16)
+    for b in range(blocks):
+        out_ref[b, 5 * rows : 5 * rows + 16, :] = both
+    scale = HEAD ** (-0.5)
+    k_t = part(1, 0, blocks).astype(jnp.float32).T.astype(jnp.bfloat16)
+    for i in range(tokens // wide):
+        first, keys = i * wide, (i + 1) * wide
+        dp = dot_nt(part(2, 0, (i + 1) * per), da_ref[first : first + wide, :])
+        p = p_ref[:keys, first : first + wide].astype(jnp.float32)
+        ds = (p * (dp - dl_ref[0:1, first : first + wide])).astype(jnp.bfloat16)
+        ds_ref[:keys, first : first + wide] = ds
+        gq = (dot_nn(k_t[:, :keys], ds) * scale).T.astype(jnp.bfloat16)
+        for j in range(per):
+            out_ref[i * per + j, 0:rows, :] = gq[j * rows : (j + 1) * rows]
+    for i in range(tokens // wide):
+        first = i * wide
+        q = part(0, i * per, blocks - i * per)
+        gk = (dot_nn(ds_ref[first : first + wide, first:], q) * scale).astype(jnp.bfloat16)
+        gv = dot_nn(p_ref[first : first + wide, first:], da_ref[first:, :]).astype(jnp.bfloat16)
+        for j in range(per):
+            out_ref[i * per + j, rows : 2 * rows, :] = gk[j * rows : (j + 1) * rows]
+            out_ref[i * per + j, 2 * rows : 3 * rows, :] = gv[j * rows : (j + 1) * rows]
+
+
+def unpack_body(rx_ref, go_ref, ct_ref, mix_ref, gq_ref, gk_ref, gv_ref, ggi_ref, ggo_ref, gf_ref, gg_ref):
+    heads = rx_ref.shape[0]
+    rows = mix_ref.shape[0]
+    groups = gf_ref.shape[0] // heads
+    group_of = lax.broadcasted_iota(jnp.int32, (groups, HEAD), 1) // (HEAD // groups)
+    gather = (group_of == lax.broadcasted_iota(jnp.int32, (groups, HEAD), 0)).astype(jnp.bfloat16)
+    for head in range(heads):
+        cols = slice(head * HEAD, (head + 1) * HEAD)
+        for at, ref in enumerate((gq_ref, gk_ref, gv_ref)):
+            ref[:, cols] = rx_ref[head, at * rows : (at + 1) * rows, :]
+        conv = rx_ref[head, 3 * rows : 4 * rows, :].astype(jnp.float32)
+        ggi_ref[:, cols] = rx_ref[head, 4 * rows : 5 * rows, :]
+        mix_ref[:, cols] = (go_ref[:, cols].astype(jnp.float32) * conv).astype(jnp.bfloat16)
+        ggo_ref[:, cols] = (ct_ref[:, cols].astype(jnp.float32) * conv).astype(jnp.bfloat16)
+        both = rx_ref[head, 5 * rows : 5 * rows + 16, :]
+        sums = dot_nt(gather, both)
+        gf_ref[head * groups : (head + 1) * groups, :] = sums[:, :FILT] + sums[:, 8 : 8 + FILT]
+        wide = both.astype(jnp.float32)
+        gg_ref[head : head + 1, :] = wide[FILT : FILT + 1] + wide[8 + FILT : 8 + FILT + 1]
+
+
+def shards_by_heads(
+    queries, key_rows, value_rows, gate_in, gate_out, kernel_taps, norm_gain, cotangent
+):
+    rows, channels = queries.shape
+    heads = channels // HEAD
+    tokens = rows * heads
+    everyone = lax.axis_size("ctx") * lax.axis_size("chan")
+    low, full = jnp.bfloat16, jnp.float32
+    gain = norm_gain.reshape(heads, HEAD)
+    (packed,) = vmem_call(pack_body, [jax.ShapeDtypeStruct((heads, 5 * rows, HEAD), low)])(
+        queries, key_rows, value_rows, gate_in, gate_out, cotangent
+    )
+    mine = lax.all_to_all(packed, "ctx", 0, 0, tiled=True)
+    probs, attn, d_mixed, partial = vmem_call(
+        functools.partial(forward_body, "ctx"),
+        [
+            jax.ShapeDtypeStruct((tokens, tokens), low),
+            jax.ShapeDtypeStruct((tokens, HEAD), low),
+            jax.ShapeDtypeStruct((tokens, HEAD), full),
+            jax.ShapeDtypeStruct((everyone, 2 * heads, rows), low),
+        ],
+        [pltpu.VMEM((tokens + 8, HEAD), full), pltpu.VMEM((2 * heads, rows), full)],
+    )(mine, kernel_taps, gain)
+    sums = lax.all_to_all(partial, ("ctx", "chan"), 0, 0, tiled=True)
+    (grads,) = vmem_call(
+        functools.partial(backward_body, "ctx", channels * lax.axis_size("chan")),
+        [jax.ShapeDtypeStruct((heads, 5 * rows + 16, HEAD), low)],
+        [
+            pltpu.VMEM((tokens + 8, HEAD), full),
+            pltpu.VMEM((tokens, tokens), low),
+            pltpu.VMEM((tokens, HEAD), low),
+            pltpu.VMEM((8, tokens), full),
+        ],
+    )(sums, mine, kernel_taps, gain, probs, attn, d_mixed)
+    back = lax.all_to_all(grads, "ctx", 0, 0, tiled=True)
+    flat = jax.ShapeDtypeStruct((rows, channels), low)
+    mixed, gq, gk, gv, ggi, ggo, gf, gg = vmem_call(
+        unpack_body,
+        [flat] * 6
+        + [
+            jax.ShapeDtypeStruct(kernel_taps.shape, full),
+            jax.ShapeDtypeStruct((heads, HEAD), full),
+        ],
+    )(back, gate_out, cotangent)
+    return (mixed, gq, gk, gv, ggi, ggo, gf, gg.reshape(channels))
+
+
+def shards(queries, *rest):
+    rows, channels = queries.shape
+    by_heads = channels // HEAD == lax.axis_size("ctx") and rows == HEAD
+    return (shards_by_heads if by_heads else shards_by_rows)(queries, *rest)
+
+
 def solution(mesh):
     placed = (
         P("ctx", "chan"),

time: 190 us -> 80.8 us (0.43)
  waiting for transfers between devices: 49.4 us -> 17.4 us
  blocking collectives: 60.7 us -> 35.2 us
  matrix products: 22.9 us -> 0 us
  local copies, waits for them, and re-layouts: 22.2 us -> 3.32 us
  Pallas kernels: 0 us -> 18.4 us
  between operations: 16.7 us -> 0.64 us
  other arithmetic: 14.8 us -> 0 us
  starting transfers between devices: 2.72 us -> 5.33 us
    all_gather x4 -> x0, waiting for transfers between devices: 49.3 us -> none  [the longest x1 26.3 us: shards(): lax.all_gather(value_rows, 'ctx', axis=0, tiled=True)]
    all_to_all x0 -> x2, blocking collectives: none -> 35.2 us  [the longest x1 22.8 us: shards_by_heads(): back = lax.all_to_all(grads, 'ctx', 0, 0, tiled=True)]
    psum x3 -> x0, blocking collectives: 34.2 us -> none  [the longest x1 14.2 us: shards(): grad_filter, grad_gain = lax.psum((tap_terms, gain_terms), 'ctx')]
    all_gather x2 -> x0, blocking collectives: 26.4 us -> none  [the longest x1 17.9 us: shards(): lax.all_gather(delta_rows, 'ctx', axis=0, tiled=True)]
    dot_general x7 -> x0, matrix products: 22.9 us -> none  [the longest x3 6.46 us: score_block(): jnp.einsum('rhe,khe->hrk', query_heads, key_block, preferred_element_type...]
    pallas_call x0 -> x4, Pallas kernels: none -> 18.4 us  [the longest x1 7.17 us: shards_by_heads(): vmem_call(functools.partial(backward_body, 'ctx', channels * lax.axis_siz...]
    all_to_all x0 -> x1, waiting for transfers between devices: none -> 17.4 us  [shards_by_heads(): mine = lax.all_to_all(packed, 'ctx', 0, 0, tiled=True)]
    convert_element_type x5 -> x0, other arithmetic: 8.45 us -> none  [the longest x1 4.02 us: shards(): grad_gate_in = (d_mixed * normed).astype(jnp.bfloat16)]
  transfers between devices with their start and end apart: 6 -> 1, of which waited for: 2 -> 1; matrix products, arithmetic and copies ran while one was open for 19% -> 1% of each run, Pallas kernels for 0% -> 0%
where the time goes in v1:
time: 80.8 us; the launch traced here: 80.3 us
  blocking collectives  35.2 us (44%)
  Pallas kernels  18.4 us (23%)
  waiting for transfers between devices  17.4 us (22%)
  starting transfers between devices  5.33 us (7%)
  local copies, waits for them, and re-layouts  3.32 us (4%)
    all_to_all x1, blocking collectives, shards_by_heads(): back = lax.all_to_all(grads, 'ctx', 0, 0, tiled=True)  22.8 us
    all_to_all x1, waiting for transfers between devices, shards_by_heads(): mine = lax.all_to_all(packed, 'ctx', 0, 0, tiled=True)  17.4 us
    all_to_all x1, blocking collectives, shards_by_heads(): sums = lax.all_to_all(partial, ('ctx', 'chan'), 0, 0, tiled=True)  12.5 us
    pallas_call x1, Pallas kernels, shards_by_heads(): vmem_call(functools.partial(backward_body, 'ctx', channels * lax.axis_siz...  7.17 us
    pallas_call x1, Pallas kernels, shards_by_heads(): vmem_call(functools.partial(forward_body, 'ctx'), [jax.ShapeDtypeStruct((...  5.71 us
    all_to_all x1, starting transfers between devices, shards_by_heads(): mine = lax.all_to_all(packed, 'ctx', 0, 0, tiled=True)  5.33 us
    unnamed x6, local copies, waits for them, and re-layouts  3.32 us
    pallas_call x1, Pallas kernels, shards_by_heads(): vmem_call(unpack_body, [flat] * 6 + [jax.ShapeDtypeStruct(kernel_taps.sha...  2.79 us
  transfers between devices with their start and end apart: 1, of which 1 were waited for; matrix products, arithmetic and copies ran while one was open for 1% of the time, Pallas kernels for 0%

profile of v1, /device:TPU:0, one launch (start us, length us, event | category | flops | bytes accessed | tf_op | source)
XLA Modules:
  0.0 80.3 jit_solution(8106966882530430879)
XLA Ops:
  0.6 2.7 %shard_map.143 = bf16[8,640,128]{2,1,0:T(8,128)(2,1)} custom-call(bf16[128,1024]{1,0:T(8,128)(2,1)} %q_ref.1, bf16[128,1024]{1,0:T(8,128)(2,1)} %k_ref.1, bf16[128,1024]{1,0:T(8,128)(2,1)} %v_ref.1, bf16[128,1024]{1,0:T(8,128)(2,1)} %gi_ref.1, bf16[128,1024]{1,0:T(8,128)(2,1)} %go_ref.3, bf16[128,1024]{1,0:T(8,128)(2,1)} %ct_ref.3), custom_call_target="tpu_custom_call" | custom-call | tf_op jit(solution)/shard_map/pallas_call | solution.py:454
  3.3 0.0 copy-start.1
  3.3 5.3 %all-to-all-start = ((bf16[8,640,128]{2,1,0:T(8,128)(2,1)}), bf16[8,640,128]{2,1,0:T(8,128)(2,1)S(1)}, u32[]{:S(2)}, u32[]{:S(2)}) async-start(bf16[8,640,128]{2,1,0:T(8,128)(2,1)} %shard_map.143), calls=%async_computation | async-start | bytes 2621440 | tf_op jit(solution)/shard_map/all_to_all | solution.py:457
  8.7 0.0 copy-done.1
  8.7 0.7 copy.16.taps_ref
  9.4 17.4 %all-to-all-done.rx_ref = bf16[8,640,128]{2,1,0:T(8,128)(2,1)S(1)} async-done(((bf16[8,640,128]{2,1,0:T(8,128)(2,1)}), bf16[8,640,128]{2,1,0:T(8,128)(2,1)S(1)}, u32[]{:S(2)}, u32[]{:S(2)}) %all-to-all-start) | async-done | bytes 1310752 | tf_op jit(solution)/shard_map/all_to_all | solution.py:457
  26.9 0.0 copy-start
  26.9 1.1 %copy-done = bf16[8,640,128]{2,1,0:T(8,128)(2,1)} copy-done((bf16[8,640,128]{2,1,0:T(8,128)(2,1)}, bf16[8,640,128]{2,1,0:T(8,128)(2,1)S(1)}, u32[]{:S(2)}) %copy-start) | copy-done | bytes 1310744
  27.9 5.7 %shard_map.144 = (bf16[1024,1024]{1,0:T(8,128)(2,1)}, bf16[1024,128]{1,0:T(8,128)(2,1)}, f32[1024,128]{1,0:T(8,128)}, bf16[32,16,128]{2,1,0:T(8,128)(2,1)}) custom-call(bf16[8,640,128]{2,1,0:T(8,128)(2,1)} %copy-done, f32[128,7]{1,0:T(8,128)} %copy.16.taps_ref, f32[8,128]{1,0:T(8,128)} %bitcast.2), custom_call_target="tpu_custom_call" | custom-call | tf_op jit(solution)/shard_map/pallas_call | solution.py:458
  33.6 12.5 %all_to_all.15.rs_ref = bf16[32,16,128]{2,1,0:T(8,128)(2,1)} all-to-all(bf16[32,16,128]{2,1,0:T(8,128)(2,1)} %get-tuple-element.20), channel_id=1, replica_groups=mesh['ctx'=8,'chan'=4] {'ctx','chan'}, dimensions={0} | all-to-all | bytes 262144 | tf_op jit(solution)/shard_map/all_to_all | solution.py:468
  46.1 7.2 %shard_map.145 = bf16[8,656,128]{2,1,0:T(8,128)(2,1)} custom-call(bf16[32,16,128]{2,1,0:T(8,128)(2,1)} %all_to_all.15.rs_ref, bf16[8,640,128]{2,1,0:T(8,128)(2,1)} %copy-done, f32[128,7]{1,0:T(8,128)} %copy.16.taps_ref, f32[8,128]{1,0:T(8,128)} %bitcast.3, bf16[1024,1024]{1,0:T(8,128)(2,1)} %get-tuple-element.21.p_ref, ...), custom_call_target="tpu_custom_call" | custom-call | tf_op jit(solution)/shard_map/pallas_call | solution.py:469
  53.3 22.8 %all_to_all.16.rx_ref = bf16[8,656,128]{2,1,0:T(8,128)(2,1)} all-to-all(bf16[8,656,128]{2,1,0:T(8,128)(2,1)} %shard_map.145), channel_id=1, replica_groups=mesh['ctx'=8,'chan'=4] {'ctx'}, dimensions={0} | all-to-all | bytes 2686976 | tf_op jit(solution)/shard_map/all_to_all | solution.py:479
  76.1 2.8 %shard_map.146 = (bf16[128,1024]{1,0:T(8,128)(2,1)}, bf16[128,1024]{1,0:T(8,128)(2,1)}, bf16[128,1024]{1,0:T(8,128)(2,1)}, bf16[128,1024]{1,0:T(8,128)(2,1)}, bf...) custom-call(bf16[8,656,128]{2,1,0:T(8,128)(2,1)} %all_to_all.16.rx_ref, ...), custom_call_target="tpu_custom_call" | custom-call | tf_op jit(solution)/shard_map/pallas_call | solution.py:481
  78.8 1.5 %copy.18 = f32[128,7]{0,1:T(8,128)} copy(f32[128,7]{1,0:T(8,128)} %get-tuple-element.38) | data formatting | bytes 7168
Async XLA Ops:
  3.3 5.3 %copy-start.1 = (f32[128,7]{0,1:T(8,128)S(1)}, f32[128,7]{0,1:T(8,128)}, u32[]{:S(2)}) copy-start(f32[128,7]{0,1:T(8,128)} %param.13) | copy-start | bytes 10756
  3.3 23.5 %all-to-all-start = ((bf16[8,640,128]{2,1,0:T(8,128)(2,1)}), bf16[8,640,128]{2,1,0:T(8,128)(2,1)S(1)}, u32[]{:S(2)}, u32[]{:S(2)}) async-start(bf16[8,640,128]{2,1,0:T(8,128)(2,1)} %shard_map.143), calls=%async_computation | async-start | bytes 2621440 | tf_op jit(solution)/shard_map/all_to_all | solution.py:457
  26.9 1.1 %copy-start = (bf16[8,640,128]{2,1,0:T(8,128)(2,1)}, bf16[8,640,128]{2,1,0:T(8,128)(2,1)S(1)}, u32[]{:S(2)}) copy-start(bf16[8,640,128]{2,1,0:T(8,128)(2,1)S(1)} %all-to-all-done.rx_ref) | copy-start | bytes 3932164
